TPU v7x, 32 devices: a whole 2x2x4 slice. The times are simulated.
32 devices in a mesh: dap: 8 (over y, x, core), dp: 4 (over z).
Axes of the slice: x: 2, y: 2, z: 4, core: 2. Of those that a mesh axis runs over, the one named last changes fastest.
Arguments:
- family_matrix: bfloat16 [512, 32, 256], P(('dp', 'dap')), parts along dimension 0, may hold values from -6 to 6
- edge_matrix: bfloat16 [128, 32, 128], P(('dp', 'dap')), parts along dimension 0, may hold values from -6 to 6
- edge_validity: int32 [128, 32], P(('dp', 'dap')), parts along dimension 0, may hold values 0 or 1
- query_key_value_gate_matrix: bfloat16 [256, 1024], replicated, may hold values from -0.375 to 0.375
- logit_offset_matrix: bfloat16 [128, 8], replicated, as said below
- heads_merge_matrix: bfloat16 [256, 256], replicated, may hold values from -0.375 to 0.375
- left_right_factor_matrix: bfloat16 [256, 64], replicated, may hold values from -0.375 to 0.375
- covariance_merge_matrix: bfloat16 [1024, 128], replicated, may hold values from -1 to 1
- edges_gate_factor_matrix: bfloat16 [128, 384], replicated, may hold values from -0.5 to 0.5
- cycle_merge_matrix: bfloat16 [128, 128], replicated, may hold values from -0.5 to 0.5
- loss_sensitivity: bfloat16 [128, 32, 128], P(('dp', 'dap')), parts along dimension 0, may hold values from -6 to 6
Outputs:
- family_after_heads: bfloat16 [512, 32, 256], P(('dp', 'dap')), parts along dimension 0
- pair_output: bfloat16 [128, 32, 128], P(('dp', 'dap')), parts along dimension 0
- pair_gradient: float32 [128, 32, 128], P(('dp', 'dap')), parts along dimension 0
There are 4 independent parts, one for each index of `dp`. A program takes and returns all parts, laid end to end along the dimension named above; an argument that names none is the same for every part. Nothing has to cross between parts.
Inputs may be any that keep to these rules, and one draw needn't show every extreme that they name: `logit_offset_matrix`: independent entries of a fixed spread clipped at four deviations.
All inputs are finite; a program needn't handle non-finite values. No bound on the sum of `edge_validity` on one device may be relied on, other than what follows from the above.
Results may differ from a plain program's by a relative error of at most 0.02.
Values may be sent and summed in bfloat16 or wider, within the bound.
No kernel may reach another device: no remote copies, remote signals or barrier semaphores. Data moves between devices by JAX's collectives and lax.ppermute only.
A program may use at most 64 MiB of HBM per device.

v0:
```python
import math
import jax
import jax.numpy as jnp
from jax import lax
from jax.sharding import PartitionSpec as P

EPSILON = 1e-05


def standardize_features(values):
    center = values - jnp.mean(values, -1, keepdims=True)
    scale_inv = lax.rsqrt(jnp.mean(center * center, -1, keepdims=True) + EPSILON)
    return center * scale_inv


def norm_back(values, grad_out):
    center = values - jnp.mean(values, -1, keepdims=True)
    scale_inv = lax.rsqrt(jnp.mean(center * center, -1, keepdims=True) + EPSILON)
    standardized_source = center * scale_inv
    return scale_inv * (
        grad_out
        - jnp.mean(grad_out, -1, keepdims=True)
        - standardized_source * jnp.mean(grad_out * standardized_source, -1, keepdims=True)
    )


def lateral_heads_mixing(
    family_shard_slice, logit_offset_whole, query_key_value_gate_matrix, heads_merge_matrix
):
    homolog_number, amino_number, feature_depth = family_shard_slice.shape
    head_count = logit_offset_whole.shape[1]
    head_size = feature_depth // head_count
    standardized_source = standardize_features(family_shard_slice.astype(jnp.float32)).astype(
        jnp.bfloat16
    )
    projected = jnp.dot(
        standardized_source.reshape(-1, feature_depth),
        query_key_value_gate_matrix,
        preferred_element_type=jnp.float32,
    )
    projected = projected.reshape(homolog_number, amino_number, 4 * feature_depth)
    shape_heads = (homolog_number, amino_number, head_count, head_size)
    queries = projected[..., :feature_depth].astype(jnp.bfloat16).reshape(shape_heads)
    key_rows = (
        projected[..., feature_depth : 2 * feature_depth].astype(jnp.bfloat16).reshape(shape_heads)
    )
    value_rows = (
        projected[..., 2 * feature_depth : 3 * feature_depth]
        .astype(jnp.bfloat16)
        .reshape(shape_heads)
    )
    gating = jax.nn.sigmoid(projected[..., 3 * feature_depth :])
    logits = jnp.einsum("sihd,sjhd->sihj", queries, key_rows, preferred_element_type=jnp.float32)
    logits = logits / math.sqrt(head_size) + logit_offset_whole.astype(jnp.float32)[None]
    weights = jax.nn.softmax(logits, axis=-1).astype(jnp.bfloat16)
    mixed = jnp.einsum("sihj,sjhd->sihd", weights, value_rows, preferred_element_type=jnp.float32)
    gated = (gating * mixed.reshape(homolog_number, amino_number, feature_depth)).astype(
        jnp.bfloat16
    )
    edge_increment = jnp.dot(
        gated.reshape(-1, feature_depth), heads_merge_matrix, preferred_element_type=jnp.float32
    )
    return (
        family_shard_slice.astype(jnp.float32)
        + edge_increment.reshape(homolog_number, amino_number, feature_depth)
    ).astype(jnp.bfloat16)


def pair_projection_step(alignment_rows, left_right_factor_matrix):
    standardized_source = standardize_features(alignment_rows.astype(jnp.float32)).astype(
        jnp.bfloat16
    )
    edge_result = jnp.dot(
        standardized_source.reshape(-1, alignment_rows.shape[2]),
        left_right_factor_matrix,
        preferred_element_type=jnp.float32,
    )
    return edge_result.reshape(alignment_rows.shape[0], alignment_rows.shape[1], -1).astype(
        jnp.bfloat16
    )


def body(
    family_matrix,
    edge_matrix,
    edge_validity,
    query_key_value_gate_matrix,
    logit_offset_matrix,
    heads_merge_matrix,
    left_right_factor_matrix,
    covariance_merge_matrix,
    edges_gate_factor_matrix,
    cycle_merge_matrix,
    loss_sensitivity,
):
    res_rows, width, pair_chans = edge_matrix.shape
    pair_normed = standardize_features(edge_matrix.astype(jnp.float32)).astype(jnp.bfloat16)
    bias_local = jnp.einsum(
        "ijc,ch->ihj", pair_normed, logit_offset_matrix, preferred_element_type=jnp.float32
    ).astype(jnp.bfloat16)
    logit_offset_whole = lax.all_gather(bias_local, "dap", axis=0, tiled=True)
    homolog_lines = family_matrix.shape[0]
    homolog_subset = math.gcd(homolog_lines, 8)
    batched_lines = family_matrix.reshape(
        homolog_lines // homolog_subset,
        homolog_subset,
        family_matrix.shape[1],
        family_matrix.shape[2],
    )
    family_after_heads = lax.map(
        lambda family_shard_slice: lateral_heads_mixing(
            family_shard_slice, logit_offset_whole, query_key_value_gate_matrix, heads_merge_matrix
        ),
        batched_lines,
    ).reshape(family_matrix.shape)
    hidden = left_right_factor_matrix.shape[1] // 2
    weight_f32 = covariance_merge_matrix.astype(jnp.float32)
    alignment_columns = lax.all_to_all(
        family_after_heads, "dap", split_axis=1, concat_axis=0, tiled=True
    )
    edge_result = pair_projection_step(alignment_columns, left_right_factor_matrix)
    left_part = edge_result[..., :hidden]
    right_part = edge_result[..., hidden:]
    sequence_full_count = alignment_columns.shape[0]
    shard_in = lax.all_gather(right_part, "dap", axis=1, tiled=True)
    outer_sum = (
        jnp.einsum("sia,sjb->ijab", left_part, shard_in, preferred_element_type=jnp.float32)
        / sequence_full_count
    )
    row_count = shard_in.shape[1]
    flat = outer_sum.reshape(res_rows * row_count, hidden * hidden)
    edge_increment = jnp.dot(flat, weight_f32, precision=lax.Precision.HIGHEST).reshape(
        res_rows, row_count, pair_chans
    )
    pair_mid = (edge_matrix.astype(jnp.float32) + edge_increment).astype(jnp.bfloat16)
    tri_normed = standardize_features(pair_mid.astype(jnp.float32)).astype(jnp.bfloat16)
    tri_proj = jnp.dot(
        tri_normed.reshape(-1, pair_chans),
        edges_gate_factor_matrix,
        preferred_element_type=jnp.float32,
    ).reshape(res_rows, width, 3 * pair_chans)
    mask_f = edge_validity.astype(jnp.float32)[..., None]
    side_a = (mask_f * tri_proj[..., :pair_chans]).astype(jnp.bfloat16)
    side_b = (mask_f * tri_proj[..., pair_chans : 2 * pair_chans]).astype(jnp.bfloat16)
    gating = jax.nn.sigmoid(tri_proj[..., 2 * pair_chans :])
    tri_prod = jnp.einsum(
        "ikc,jkc->ijc",
        side_a,
        lax.all_gather(side_b, "dap", axis=0, tiled=True),
        preferred_element_type=jnp.float32,
    )
    prod_normed = standardize_features(tri_prod).astype(jnp.bfloat16)
    tri_update = jnp.dot(
        prod_normed.reshape(-1, pair_chans), cycle_merge_matrix, preferred_element_type=jnp.float32
    ).reshape(res_rows, width, pair_chans)
    pair_output = (pair_mid.astype(jnp.float32) + gating * tri_update).astype(jnp.bfloat16)
    cot_f32 = loss_sensitivity.astype(jnp.float32)
    grad_update = (cot_f32 * gating).astype(jnp.bfloat16)
    grad_normed = jnp.dot(
        grad_update.reshape(-1, pair_chans),
        cycle_merge_matrix.T,
        preferred_element_type=jnp.float32,
    ).reshape(res_rows, width, pair_chans)
    grad_prod = norm_back(tri_prod, grad_normed).astype(jnp.bfloat16)
    grad_part = grad_prod
    grad_a = jnp.einsum(
        "ijc,jkc->ikc",
        grad_part,
        lax.all_gather(side_b, "dap", axis=0, tiled=True),
        preferred_element_type=jnp.float32,
    )
    grad_part = grad_prod
    grad_b = lax.psum_scatter(
        jnp.einsum("ijc,ikc->jkc", grad_part, side_a, preferred_element_type=jnp.float32).astype(
            jnp.bfloat16
        ),
        "dap",
        scatter_dimension=0,
        tiled=True,
    ).astype(jnp.float32)
    grad_gate = cot_f32 * tri_update * gating * (1.0 - gating)
    grad_proj = jnp.concatenate([mask_f * grad_a, mask_f * grad_b, grad_gate], -1).astype(
        jnp.bfloat16
    )
    grad_input = jnp.dot(
        grad_proj.reshape(-1, 3 * pair_chans),
        edges_gate_factor_matrix.T,
        preferred_element_type=jnp.float32,
    ).reshape(res_rows, width, pair_chans)
    pair_gradient = cot_f32 + norm_back(pair_mid.astype(jnp.float32), grad_input)
    return (family_after_heads, pair_output, pair_gradient)


def solution(mesh):
    in_specs = (
        P(("dp", "dap"), None, None),
        P(("dp", "dap"), None, None),
        P(("dp", "dap"), None),
        P(),
        P(),
        P(),
        P(),
        P(),
        P(),
        P(),
        P(("dp", "dap"), None, None),
    )
    out_specs = (
        P(("dp", "dap"), None, None),
        P(("dp", "dap"), None, None),
        P(("dp", "dap"), None, None),
    )
    return jax.shard_map(body, mesh=mesh, in_specs=in_specs, out_specs=out_specs, check_vma=False)
```

profile of v0, /device:TPU:0, one launch (start us, length us, event | category | flops | bytes accessed | tf_op | source)
XLA Modules:
  0.0 126.4 jit_solution(6555764046027350197)
XLA Ops:
  10.0 10.7 %all_gather.10 = bf16[32,8,32]{2,1,0:T(8,128)(2,1)S(1)} all-gather(bf16[4,8,32]{2,1,0:T(8,128)(2,1)S(1)} %fusion.36), channel_id=1, replica_groups=mesh['dap'=8,'dp'=4] {'dap'}, dimensions={0}, use_global_device_ids=true | all-gather | bytes 18432 | tf_op jit(solution)/shard_map/all_gather | solution.py:101
  20.8 20.3 %while.10 = (s32[]{:T(128)}, bf16[2,8,32,256]{3,2,1,0:T(8,128)(2,1)}, bf16[2,8,32,256]{3,2,1,0:T(8,128)(2,1)}, bf16[256,1024]{1,0:T(8,128)(2,1)}, bf16[32,8,32]{...) while((s32[]{:T(128)}, bf16[2,8,32,256]{3,2,1,0:T(8,128)(2,1)}, ...), condition=%wide.region_7.8_spmd, body=%wide.region_2.7_spmd.sunk | while | flops 178071872 | bytes 7186573 | solution.py:110
  20.9 1.0 convert_reduce_fusion.3
  21.9 1.1 fusion.126
  23.0 1.5 %fusion.127 = (bf16[8,32,1024]{2,1,0:T(8,128)(2,1)S(1)}, f32[8,32,1024]{2,1,0:T(8,128)S(1)}) fusion(bf16[256,1024]{1,0:T(8,128)(2,1)} %get-tuple-element.193, f32[8,32]{1,0:T(8,128)S(1)} %add_rsqrt_fusion.5, f32[8,32]{1,0:T(8,128)S(1)} %broadcast_multiply_fusion.9, bf16[2,8,32,256]{3,2,1,0:T(8,128)(2,1)} %get-tuple-element.192, s32[]{:T(128)} %get-tuple-element.183), kind=kOutput, calls=%fused_computation.130.clone.1 | convolution fusion | flops 134742016 | bytes 2230784 | tf_op jit(solution)/shard_map/while/body/eval_jaxpr/dot_general | solution.py:36
  26.4 1.0 copy.176
  27.4 1.4 %fusion.131 = f32[8,8,32,32]{3,2,1,0:T(8,128)S(1)} fusion(bf16[8,32,8,32]{1,3,2,0:T(8,128)(2,1)} %bitcast.148, f32[8,32,8]{1,2,0:T(8,128)} %fusion.130, f32[8,32,8,32]{1,3,2,0:T(8,128)S(1)} %fusion.129), kind=kOutput, calls=%fused_computation.11.clone.1 | convolution fusion | flops 4392991 | bytes 663552 | tf_op jit(solution)/shard_map/while/body/eval_jaxpr/sihj,sjhd->sihd/dot_general | solution.py:56
  29.1 1.8 %fusion.132 = bf16[2,8,32,256]{3,2,1,0:T(8,128)(2,1)} fusion(bf16[2,8,32,256]{3,2,1,0:T(8,128)(2,1)} %get-tuple-element.184, s32[]{:T(128)} %get-tuple-element.183, f32[8,32,256]{2,1,0:T(8,128)S(1)} %copy.177, f32[8,32,1024]{2,1,0:T(8,128)S(1)} %get-tuple-element.175, bf16[256,256]{1,0:T(8,128)(2,1)} %get-tuple-element.195, ...), kind=kOutput, calls=%fused_computation.9.clone.1 | convolution fusion | flops 34078720 | bytes 918016 | tf_op jit(solution)/shard_map/while/body/eval_jaxpr/dot_general | solution.py:60
  31.0 1.0 convert_reduce_fusion.3
  32.0 1.1 fusion.126
  33.2 1.5 %fusion.127 = (bf16[8,32,1024]{2,1,0:T(8,128)(2,1)S(1)}, f32[8,32,1024]{2,1,0:T(8,128)S(1)}) fusion(bf16[256,1024]{1,0:T(8,128)(2,1)} %get-tuple-element.193, f32[8,32]{1,0:T(8,128)S(1)} %add_rsqrt_fusion.5, f32[8,32]{1,0:T(8,128)S(1)} %broadcast_multiply_fusion.9, bf16[2,8,32,256]{3,2,1,0:T(8,128)(2,1)} %get-tuple-element.192, s32[]{:T(128)} %get-tuple-element.183), kind=kOutput, calls=%fused_computation.130.clone.1 | convolution fusion | flops 134742016 | bytes 2230784 | tf_op jit(solution)/shard_map/while/body/eval_jaxpr/dot_general | solution.py:36
  36.5 1.0 copy.176
  37.5 1.4 %fusion.131 = f32[8,8,32,32]{3,2,1,0:T(8,128)S(1)} fusion(bf16[8,32,8,32]{1,3,2,0:T(8,128)(2,1)} %bitcast.148, f32[8,32,8]{1,2,0:T(8,128)} %fusion.130, f32[8,32,8,32]{1,3,2,0:T(8,128)S(1)} %fusion.129), kind=kOutput, calls=%fused_computation.11.clone.1 | convolution fusion | flops 4392991 | bytes 663552 | tf_op jit(solution)/shard_map/while/body/eval_jaxpr/sihj,sjhd->sihd/dot_general | solution.py:56
  39.3 1.8 %fusion.132 = bf16[2,8,32,256]{3,2,1,0:T(8,128)(2,1)} fusion(bf16[2,8,32,256]{3,2,1,0:T(8,128)(2,1)} %get-tuple-element.184, s32[]{:T(128)} %get-tuple-element.183, f32[8,32,256]{2,1,0:T(8,128)S(1)} %copy.177, f32[8,32,1024]{2,1,0:T(8,128)S(1)} %get-tuple-element.175, bf16[256,256]{1,0:T(8,128)(2,1)} %get-tuple-element.195, ...), kind=kOutput, calls=%fused_computation.9.clone.1 | convolution fusion | flops 34078720 | bytes 918016 | tf_op jit(solution)/shard_map/while/body/eval_jaxpr/dot_general | solution.py:60
  41.1 1.8 %copy.169 = bf16[2,8,32,256]{3,1,0,2:T(8,128)(2,1)} copy(bf16[2,8,32,256]{3,2,1,0:T(8,128)(2,1)} %get-tuple-element.35) | data formatting | bytes 524288 | tf_op jit(solution)/shard_map/while | solution.py:110
  42.9 3.4 %all-to-all-start = ((bf16[16,32,256]{2,0,1:T(8,128)(2,1)}), bf16[16,32,256]{2,0,1:T(8,128)(2,1)S(1)}, u32[]{:S(2)}, u32[]{:S(2)}) async-start(bf16[16,32,256]{2,0,1:T(8,128)(2,1)} %bitcast.121), calls=%async_computation | async-start | bytes 524288 | tf_op jit(solution)/shard_map/all_to_all | solution.py:118
  46.4 6.8 %all-to-all-done = bf16[16,32,256]{2,0,1:T(8,128)(2,1)S(1)} async-done(((bf16[16,32,256]{2,0,1:T(8,128)(2,1)}), bf16[16,32,256]{2,0,1:T(8,128)(2,1)S(1)}, u32[]{:S(2)}, u32[]{:S(2)}) %all-to-all-start) | async-done | bytes 262176 | tf_op jit(solution)/shard_map/all_to_all | solution.py:118
  54.4 8.4 %all_gather.11 = bf16[128,32,32]{0,2,1:T(8,128)(2,1)S(1)} all-gather(bf16[128,4,32]{0,2,1:T(8,128)(2,1)S(1)} %slice.39), channel_id=1, replica_groups=mesh['dap'=8,'dp'=4] {'dap'}, dimensions={1}, use_global_device_ids=true | all-gather | bytes 294912 | tf_op jit(solution)/shard_map/all_gather | solution.py:125
  62.7 1.8 %multiply_bitcast_fusion = f32[4,32,32,32]{2,3,0,1:T(8,128)} fusion(bf16[128,32,32]{0,2,1:T(8,128)(2,1)S(1)} %all_gather.11, bf16[128,4,64]{0,2,1:T(8,128)(2,1)S(1)} %convolution_convert_fusion), kind=kOutput, calls=%fused_computation.40 | convolution fusion | flops 33685504 | bytes 819200 | tf_op jit(solution)/shard_map/sia,sjb->ijab/dot_general | solution.py:127
  64.5 1.9 %copy.138 = f32[4,32,32,32]{3,2,1,0:T(8,128)S(1)} copy(f32[4,32,32,32]{2,3,0,1:T(8,128)} %multiply_bitcast_fusion) | data formatting | bytes 1048576 | tf_op jit(solution)/shard_map/div | solution.py:127
  68.5 9.5 %all_gather.12 = bf16[32,32,128]{2,1,0:T(8,128)(2,1)S(1)} all-gather(bf16[4,32,128]{2,1,0:T(8,128)(2,1)S(1)} %get-tuple-element.117), channel_id=1, replica_groups=mesh['dap'=8,'dp'=4] {'dap'}, dimensions={0}, use_global_device_ids=true | all-gather | bytes 294912 | tf_op jit(solution)/shard_map/all_gather | solution.py:149
  77.9 1.4 %copy.139 = bf16[32,32,128]{1,0,2:T(8,128)(2,1)S(1)} copy(bf16[32,32,128]{2,1,0:T(8,128)(2,1)S(1)} %all_gather.12) | data formatting | bytes 524288 | tf_op jit(solution)/shard_map/all_gather | solution.py:149
  81.6 2.0 %copy.147 = bf16[128,32,32]{0,1,2:T(8,128)(2,1)} copy(bf16[128,32,32]{2,1,0:T(8,128)(2,1)S(1)} %fusion.93) | data formatting | bytes 524288 | tf_op jit(solution)/shard_map/ijc,ikc->jkc/dot_general | solution.py:174
  84.9 32.7 %reduce-scatter.2.cloned.1.call-done = bf16[4,32,128]{2,1,0:T(8,128)(2,1)} async-done(((bf16[32,32,128]{2,1,0:T(8,128)(2,1)}), bf16[4,32,128]{2,1,0:T(8,128)(2,1)}) %reduce-scatter.2.cloned.1.call-update) | async-done | bytes 32784 | tf_op jit(solution)/shard_map/reduce_scatter | solution.py:173
  (88 shorter events, 15.7 us)
Async XLA Ops:
  7.2 60.3 %copy-start = (bf16[1024,128]{1,0:T(8,128)(2,1)S(1)}, bf16[1024,128]{1,0:T(8,128)(2,1)}, u32[]{:S(2)}) copy-start(bf16[1024,128]{1,0:T(8,128)(2,1)} %param.20) | copy-start | bytes 786436
  20.8 25.6 %copy-start.7 = (s32[4,32]{1,0:T(4,128)S(1)}, s32[4,32]{1,0:T(4,128)}, u32[]{:S(2)}) copy-start(s32[4,32]{1,0:T(4,128)} %param.15) | copy-start | bytes 1540
  20.8 4.2 %copy-start.1 = (bf16[32,8,32]{0,2,1:T(8,128)(2,1)}, bf16[32,8,32]{0,2,1:T(8,128)(2,1)S(1)}, u32[]{:S(2)}) copy-start(bf16[32,8,32]{0,2,1:T(8,128)(2,1)S(1)} %get-tuple-element.194) | copy-start | bytes 49156 | tf_op jit(solution)/shard_map/while
  28.8 2.2 %copy-start.2 = (bf16[32,8,32]{0,2,1:T(8,128)(2,1)S(1)}, bf16[32,8,32]{0,2,1:T(8,128)(2,1)}, u32[]{:S(2)}) copy-start(bf16[32,8,32]{0,2,1:T(8,128)(2,1)} %copy-done.1) | copy-start | bytes 49156 | tf_op jit(solution)/shard_map/while
  31.0 4.2 %copy-start.1 = (bf16[32,8,32]{0,2,1:T(8,128)(2,1)}, bf16[32,8,32]{0,2,1:T(8,128)(2,1)S(1)}, u32[]{:S(2)}) copy-start(bf16[32,8,32]{0,2,1:T(8,128)(2,1)S(1)} %get-tuple-element.194) | copy-start | bytes 49156 | tf_op jit(solution)/shard_map/while
  39.0 2.2 %copy-start.2 = (bf16[32,8,32]{0,2,1:T(8,128)(2,1)S(1)}, bf16[32,8,32]{0,2,1:T(8,128)(2,1)}, u32[]{:S(2)}) copy-start(bf16[32,8,32]{0,2,1:T(8,128)(2,1)} %copy-done.1) | copy-start | bytes 49156 | tf_op jit(solution)/shard_map/while
  41.1 13.0 %copy-start.5 = (bf16[256,64]{0,1:T(8,128)(2,1)S(1)}, bf16[256,64]{0,1:T(8,128)(2,1)}, u32[]{:S(2)}) copy-start(bf16[256,64]{0,1:T(8,128)(2,1)} %param.19) | copy-start | bytes 98308
  42.9 10.3 %all-to-all-start = ((bf16[16,32,256]{2,0,1:T(8,128)(2,1)}), bf16[16,32,256]{2,0,1:T(8,128)(2,1)S(1)}, u32[]{:S(2)}, u32[]{:S(2)}) async-start(bf16[16,32,256]{2,0,1:T(8,128)(2,1)} %bitcast.121), calls=%async_computation | async-start | bytes 524288 | tf_op jit(solution)/shard_map/all_to_all | solution.py:118
  46.3 71.3 %reduce-scatter.2.cloned.1.call-start = ((), (), s32[]{:S(2)}) async-start(), calls=%async_computation.2 | async-start | bytes 294912 | tf_op jit(solution)/shard_map/reduce_scatter | solution.py:173
  66.5 1.0 copy-start.3
  66.5 1.6 %copy-start.4 = (bf16[128,384]{1,0:T(8,128)(2,1)S(1)}, bf16[128,384]{1,0:T(8,128)(2,1)}, u32[]{:S(2)}) copy-start(bf16[128,384]{1,0:T(8,128)(2,1)} %param.21) | copy-start | bytes 294916
  67.9 12.3 %copy-start.6 = (bf16[4,32,128]{2,1,0:T(8,128)(2,1)S(1)}, bf16[4,32,128]{2,1,0:T(8,128)(2,1)}, u32[]{:S(2)}) copy-start(bf16[4,32,128]{2,1,0:T(8,128)(2,1)} %param.23) | copy-start | bytes 98308
  67.9 12.3 %copy-start.8 = (bf16[128,128]{1,0:T(8,128)(2,1)S(1)}, bf16[128,128]{1,0:T(8,128)(2,1)}, u32[]{:S(2)}) copy-start(bf16[128,128]{1,0:T(8,128)(2,1)} %param.22) | copy-start | bytes 98308
Sparse Core Ops, SparseCore 0:
  83.7 33.8 reduce-scatter.1
where the time goes:
time: 127 us; the launch traced here: 126 us
  waiting for transfers between devices  39.5 us (31%)
  blocking collectives  28.5 us (22%)
  matrix products  16.8 us (13%)
  between operations  14.3 us (11%)
  local copies, waits for them, and re-layouts  12.5 us (10%)
  other arithmetic  11 us (9%)
  starting transfers between devices  3.45 us (3%)
    reduce_scatter x1, waiting for transfers between devices, body(): lax.psum_scatter(jnp.einsum('ijc,ikc->jkc', grad_part, side_a, preferred_...  32.7 us
    all_gather x1, blocking collectives, body(): logit_offset_whole = lax.all_gather(bias_local, 'dap', axis=0, tiled=True)  10.7 us
    all_gather x1, blocking collectives, body(): lax.all_gather(side_b, 'dap', axis=0, tiled=True)  9.47 us
    all_gather x1, blocking collectives, body(): shard_in = lax.all_gather(right_part, 'dap', axis=1, tiled=True)  8.35 us
    all_to_all x1, waiting for transfers between devices, body(): lax.all_to_all(family_after_heads, 'dap', split_axis=1, concat_axis=0, ti...  6.8 us
    dot_general x2, matrix products, lateral_heads_mixing(): jnp.dot(gated.reshape(-1, feature_depth), heads_merge_matrix, preferred_e...  3.69 us
    reduce_sum x6, other arithmetic, standardize_features(): jnp.mean(center * center, -1, keepdims=True) + EPSILON  3.67 us
    all_to_all x1, starting transfers between devices, body(): lax.all_to_all(family_after_heads, 'dap', split_axis=1, concat_axis=0, ti...  3.41 us
  transfers between devices with their start and end apart: 2, of which 2 were waited for; matrix products, arithmetic and copies ran while one was open for 1% of the time, Pallas kernels for 0%

commit v1 on v0

--- a/solution.py
+++ b/solution.py
@@ -5,6 +5,28 @@
 from jax.sharding import PartitionSpec as P
 
 EPSILON = 1e-05
+
+
+def in_order(blocks, dim):
+    shape = list(blocks.shape[1:])
+    shape[dim] *= blocks.shape[0]
+    return jnp.moveaxis(blocks, 0, dim).reshape(shape)
+
+
+def gather_around(x, axis, dim):
+    peers = lax.axis_size(axis)
+    pairs = [(i, (i + 1) % peers) for i in range(peers)]
+    back = [(b, a) for a, b in pairs]
+    lower, upper = ([], [])
+    for step in range(peers - 1):
+        if step % 2 == 0:
+            lower.append(lax.ppermute(lower[-1] if lower else x, axis, pairs))
+        else:
+            upper.append(lax.ppermute(upper[-1] if upper else x, axis, back))
+    blocks = jnp.stack([*lower[::-1], x, *upper])
+    shift = lax.axis_index(axis) - len(lower)
+    blocks = blocks[(jnp.arange(peers) - shift) % peers]
+    return in_order(blocks, dim)
 
 
 def standardize_features(values):
@@ -144,10 +166,7 @@
     side_b = (mask_f * tri_proj[..., pair_chans : 2 * pair_chans]).astype(jnp.bfloat16)
     gating = jax.nn.sigmoid(tri_proj[..., 2 * pair_chans :])
     tri_prod = jnp.einsum(
-        "ikc,jkc->ijc",
-        side_a,
-        lax.all_gather(side_b, "dap", axis=0, tiled=True),
-        preferred_element_type=jnp.float32,
+        "ikc,jkc->ijc", side_a, gather_around(side_b, "dap", 0), preferred_element_type=jnp.float32
     )
     prod_normed = standardize_features(tri_prod).astype(jnp.bfloat16)
     tri_update = jnp.dot(

time: 127 us -> 146 us (1.15)
  waiting for transfers between devices: 39.5 us -> 49 us
  starting transfers between devices: 3.45 us -> 10.8 us
  local copies, waits for them, and re-layouts: 12.5 us -> 14.6 us
    ppermute x0 -> x7, waiting for transfers between devices: none -> 8.27 us  [the longest x4 6.76 us: gather_around(): lower.append(lax.ppermute(lower[-1] if lower else x, axis, pairs))]
    ppermute x0 -> x7, starting transfers between devices: none -> 7.39 us  [the longest x3 6.98 us: gather_around(): upper.append(lax.ppermute(upper[-1] if upper else x, axis, back))]
  transfers between devices with their start and end apart: 2 -> 9, of which waited for: 2 -> 6; matrix products, arithmetic and copies ran while one was open for 1% -> 2% of each run, Pallas kernels for 0% -> 0%
where the time goes in v1:
time: 146 us; the launch traced here: 145 us
  waiting for transfers between devices  49 us (34%)
  blocking collectives  28.4 us (19%)
  matrix products  16.8 us (12%)
  local copies, waits for them, and re-layouts  14.6 us (10%)
  between operations  14.4 us (10%)
  other arithmetic  11 us (8%)
  starting transfers between devices  10.8 us (7%)
    reduce_scatter x1, waiting for transfers between devices, body(): lax.psum_scatter(jnp.einsum('ijc,ikc->jkc', grad_part, side_a, preferred_...  33.9 us
    all_gather x1, blocking collectives, body(): logit_offset_whole = lax.all_gather(bias_local, 'dap', axis=0, tiled=True)  10.7 us
    all_gather x1, blocking collectives, body(): lax.all_gather(side_b, 'dap', axis=0, tiled=True)  9.35 us
    all_gather x1, blocking collectives, body(): shard_in = lax.all_gather(right_part, 'dap', axis=1, tiled=True)  8.35 us
    ppermute x3, starting transfers between devices, gather_around(): upper.append(lax.ppermute(upper[-1] if upper else x, axis, back))  6.98 us
    all_to_all x1, waiting for transfers between devices, body(): lax.all_to_all(family_after_heads, 'dap', split_axis=1, concat_axis=0, ti...  6.79 us
    ppermute x4, waiting for transfers between devices, gather_around(): lower.append(lax.ppermute(lower[-1] if lower else x, axis, pairs))  6.76 us
    dot_general x2, matrix products, lateral_heads_mixing(): jnp.dot(gated.reshape(-1, feature_depth), heads_merge_matrix, preferred_e...  3.69 us
  transfers between devices with their start and end apart: 9, of which 6 were waited for; matrix products, arithmetic and copies ran while one was open for 2% of the time, Pallas kernels for 0%

profile of v1, /device:TPU:0, one launch (start us, length us, event | category | flops | bytes accessed | tf_op | source)
XLA Modules:
  0.0 145.4 jit_solution(12423252072178044105)
XLA Ops:
  10.0 10.7 %all_gather.9 = bf16[32,8,32]{2,1,0:T(8,128)(2,1)S(1)} all-gather(bf16[4,8,32]{2,1,0:T(8,128)(2,1)S(1)} %fusion.36), channel_id=1, replica_groups=mesh['dap'=8,'dp'=4] {'dap'}, dimensions={0}, use_global_device_ids=true | all-gather | bytes 18432 | tf_op jit(solution)/shard_map/all_gather | solution.py:123
  20.8 20.3 %while.10 = (s32[]{:T(128)}, bf16[2,8,32,256]{3,2,1,0:T(8,128)(2,1)}, bf16[2,8,32,256]{3,2,1,0:T(8,128)(2,1)}, bf16[256,1024]{1,0:T(8,128)(2,1)}, bf16[32,8,32]{...) while((s32[]{:T(128)}, bf16[2,8,32,256]{3,2,1,0:T(8,128)(2,1)}, ...), condition=%wide.region_7.8_spmd, body=%wide.region_2.7_spmd.sunk | while | flops 178071872 | bytes 7186573 | solution.py:132
  23.0 1.5 %fusion.129 = (bf16[8,32,1024]{2,1,0:T(8,128)(2,1)S(1)}, f32[8,32,1024]{2,1,0:T(8,128)S(1)}) fusion(bf16[256,1024]{1,0:T(8,128)(2,1)} %get-tuple-element.193, f32[8,32]{1,0:T(8,128)S(1)} %add_rsqrt_fusion.5, f32[8,32]{1,0:T(8,128)S(1)} %broadcast_multiply_fusion.9, bf16[2,8,32,256]{3,2,1,0:T(8,128)(2,1)} %get-tuple-element.192, s32[]{:T(128)} %get-tuple-element.183), kind=kOutput, calls=%fused_computation.146.clone.1 | convolution fusion | flops 134742016 | bytes 2230784 | tf_op jit(solution)/shard_map/while/body/eval_jaxpr/dot_general | solution.py:58
  29.1 1.8 %fusion.134 = bf16[2,8,32,256]{3,2,1,0:T(8,128)(2,1)} fusion(bf16[2,8,32,256]{3,2,1,0:T(8,128)(2,1)} %get-tuple-element.184, s32[]{:T(128)} %get-tuple-element.183, f32[8,32,256]{2,1,0:T(8,128)S(1)} %copy.177, f32[8,32,1024]{2,1,0:T(8,128)S(1)} %get-tuple-element.175, bf16[256,256]{1,0:T(8,128)(2,1)} %get-tuple-element.195, ...), kind=kOutput, calls=%fused_computation.10.clone.1 | convolution fusion | flops 34078720 | bytes 918016 | tf_op jit(solution)/shard_map/while/body/eval_jaxpr/dot_general | solution.py:82
  33.2 1.5 %fusion.129 = (bf16[8,32,1024]{2,1,0:T(8,128)(2,1)S(1)}, f32[8,32,1024]{2,1,0:T(8,128)S(1)}) fusion(bf16[256,1024]{1,0:T(8,128)(2,1)} %get-tuple-element.193, f32[8,32]{1,0:T(8,128)S(1)} %add_rsqrt_fusion.5, f32[8,32]{1,0:T(8,128)S(1)} %broadcast_multiply_fusion.9, bf16[2,8,32,256]{3,2,1,0:T(8,128)(2,1)} %get-tuple-element.192, s32[]{:T(128)} %get-tuple-element.183), kind=kOutput, calls=%fused_computation.146.clone.1 | convolution fusion | flops 134742016 | bytes 2230784 | tf_op jit(solution)/shard_map/while/body/eval_jaxpr/dot_general | solution.py:58
  37.5 1.4 fusion.133
  39.3 1.8 %fusion.134 = bf16[2,8,32,256]{3,2,1,0:T(8,128)(2,1)} fusion(bf16[2,8,32,256]{3,2,1,0:T(8,128)(2,1)} %get-tuple-element.184, s32[]{:T(128)} %get-tuple-element.183, f32[8,32,256]{2,1,0:T(8,128)S(1)} %copy.177, f32[8,32,1024]{2,1,0:T(8,128)S(1)} %get-tuple-element.175, bf16[256,256]{1,0:T(8,128)(2,1)} %get-tuple-element.195, ...), kind=kOutput, calls=%fused_computation.10.clone.1 | convolution fusion | flops 34078720 | bytes 918016 | tf_op jit(solution)/shard_map/while/body/eval_jaxpr/dot_general | solution.py:82
  41.1 1.8 %copy.169 = bf16[2,8,32,256]{3,1,0,2:T(8,128)(2,1)} copy(bf16[2,8,32,256]{3,2,1,0:T(8,128)(2,1)} %get-tuple-element.35) | data formatting | bytes 524288 | tf_op jit(solution)/shard_map/while | solution.py:132
  42.9 3.4 %all-to-all-start = ((bf16[16,32,256]{2,0,1:T(8,128)(2,1)}), bf16[16,32,256]{2,0,1:T(8,128)(2,1)S(1)}, u32[]{:S(2)}, u32[]{:S(2)}) async-start(bf16[16,32,256]{2,0,1:T(8,128)(2,1)} %bitcast.140), calls=%async_computation | async-start | bytes 524288 | tf_op jit(solution)/shard_map/all_to_all | solution.py:140
  46.4 6.8 %all-to-all-done = bf16[16,32,256]{2,0,1:T(8,128)(2,1)S(1)} async-done(((bf16[16,32,256]{2,0,1:T(8,128)(2,1)}), bf16[16,32,256]{2,0,1:T(8,128)(2,1)S(1)}, u32[]{:S(2)}, u32[]{:S(2)}) %all-to-all-start) | async-done | bytes 262176 | tf_op jit(solution)/shard_map/all_to_all | solution.py:140
  54.4 8.4 %all_gather.10 = bf16[128,32,32]{0,2,1:T(8,128)(2,1)S(1)} all-gather(bf16[128,4,32]{0,2,1:T(8,128)(2,1)S(1)} %slice.41), channel_id=1, replica_groups=mesh['dap'=8,'dp'=4] {'dap'}, dimensions={1}, use_global_device_ids=true | all-gather | bytes 294912 | tf_op jit(solution)/shard_map/all_gather | solution.py:147
  62.7 1.8 %multiply_bitcast_fusion = f32[4,32,32,32]{2,3,0,1:T(8,128)} fusion(bf16[128,32,32]{0,2,1:T(8,128)(2,1)S(1)} %all_gather.10, bf16[128,4,64]{0,2,1:T(8,128)(2,1)S(1)} %convolution_convert_fusion), kind=kOutput, calls=%fused_computation.41 | convolution fusion | flops 33685504 | bytes 819200 | tf_op jit(solution)/shard_map/sia,sjb->ijab/dot_general | solution.py:149
  64.5 1.9 %copy.138 = f32[4,32,32,32]{3,2,1,0:T(8,128)S(1)} copy(f32[4,32,32,32]{2,3,0,1:T(8,128)} %multiply_bitcast_fusion) | data formatting | bytes 1048576 | tf_op jit(solution)/shard_map/div | solution.py:149
  68.9 3.9 %collective-permute-done = bf16[4,32,128]{2,1,0:T(8,128)(2,1)S(1)} collective-permute-done((bf16[4,32,128]{2,1,0:T(8,128)(2,1)S(1)}, bf16[4,32,128]{2,1,0:T(8,128)(2,1)S(1)}, u32[]{:S(2)}, u32[]{:S(2)}) %collective-permute-start) | collective-permute-done | bytes 32800 | tf_op jit(solution)/shard_map/ppermute | solution.py:23
  72.8 2.6 %collective-permute-start.4 = (bf16[4,32,128]{2,1,0:T(8,128)(2,1)S(1)}, bf16[4,32,128]{2,1,0:T(8,128)(2,1)S(1)}, u32[]{:S(2)}, u32[]{:S(2)}) collective-permute-start(bf16[4,32,128]{2,1,0:T(8,128)(2,1)S(1)} %get-tuple-element.117), channel_id=1, source_target_pairs={{4,0},{8,4},{12,8},{16,12},{20,16},{24,20},{28,24},{0,28},{5,1},{9... | collective-permute-start | bytes 98312 | tf_op jit(solution)/shard_map/ppermute | solution.py:25
  75.4 1.9 %collective-permute-done.1 = bf16[4,32,128]{2,1,0:T(8,128)(2,1)S(1)} collective-permute-done((bf16[4,32,128]{2,1,0:T(8,128)(2,1)S(1)}, bf16[4,32,128]{2,1,0:T(8,128)(2,1)S(1)}, u32[]{:S(2)}, u32[]{:S(2)}) %collective-permute-start.1) | collective-permute-done | bytes 32800 | tf_op jit(solution)/shard_map/ppermute | solution.py:23
  77.9 2.7 %collective-permute-start.5 = (bf16[4,32,128]{2,1,0:T(8,128)(2,1)S(1)}, bf16[4,32,128]{2,1,0:T(8,128)(2,1)S(1)}, u32[]{:S(2)}, u32[]{:S(2)}) collective-permute-start(bf16[4,32,128]{2,1,0:T(8,128)(2,1)S(1)} %collective-permute-done.4), channel_id=1, source_target_pairs={{4,0},{8,4},{12,8},{16,12},{20,16},{24,20},{28,24},{0,28},{5,1},{9... | collective-permute-start | bytes 98312 | tf_op jit(solution)/shard_map/ppermute | solution.py:25
  81.6 9.4 %all_gather.11 = bf16[32,32,128]{2,1,0:T(8,128)(2,1)S(1)} all-gather(bf16[4,32,128]{2,1,0:T(8,128)(2,1)S(1)} %get-tuple-element.117), channel_id=1, replica_groups=mesh['dap'=8,'dp'=4] {'dap'}, dimensions={0}, use_global_device_ids=true | all-gather | bytes 294912 | tf_op jit(solution)/shard_map/all_gather | solution.py:188
  90.9 1.4 copy.144
  92.4 1.6 %collective-permute-start.6 = (bf16[4,32,128]{2,1,0:T(8,128)(2,1)S(1)}, bf16[4,32,128]{2,1,0:T(8,128)(2,1)S(1)}, u32[]{:S(2)}, u32[]{:S(2)}) collective-permute-start(bf16[4,32,128]{2,1,0:T(8,128)(2,1)S(1)} %collective-permute-done.5), channel_id=1, source_target_pairs={{4,0},{8,4},{12,8},{16,12},{20,16},{24,20},{28,24},{0,28},{5,1},{9... | collective-permute-start | bytes 98312 | tf_op jit(solution)/shard_map/ppermute | solution.py:25
  94.1 1.5 %collective-permute-done.6 = bf16[4,32,128]{2,1,0:T(8,128)(2,1)S(1)} collective-permute-done((bf16[4,32,128]{2,1,0:T(8,128)(2,1)S(1)}, bf16[4,32,128]{2,1,0:T(8,128)(2,1)S(1)}, u32[]{:S(2)}, u32[]{:S(2)}) %collective-permute-start.6) | collective-permute-done | bytes 32800 | tf_op jit(solution)/shard_map/ppermute | solution.py:25
  96.2 1.4 copy.139
  99.3 2.0 %copy.147 = bf16[128,32,32]{0,1,2:T(8,128)(2,1)} copy(bf16[128,32,32]{2,1,0:T(8,128)(2,1)S(1)} %fusion.95) | data formatting | bytes 524288 | tf_op jit(solution)/shard_map/ijc,ikc->jkc/dot_general | solution.py:193
  102.7 33.9 %reduce-scatter.2.cloned.1.call-done = bf16[4,32,128]{2,1,0:T(8,128)(2,1)} async-done(((bf16[32,32,128]{2,1,0:T(8,128)(2,1)}), bf16[4,32,128]{2,1,0:T(8,128)(2,1)}) %reduce-scatter.2.cloned.1.call-update) | async-done | bytes 32784 | tf_op jit(solution)/shard_map/reduce_scatter | solution.py:192
  (114 shorter events, 25.5 us)
Async XLA Ops:
  7.2 60.3 %copy-start = (bf16[1024,128]{1,0:T(8,128)(2,1)S(1)}, bf16[1024,128]{1,0:T(8,128)(2,1)}, u32[]{:S(2)}) copy-start(bf16[1024,128]{1,0:T(8,128)(2,1)} %param.20) | copy-start | bytes 786436
  20.8 25.6 %copy-start.7 = (s32[4,32]{1,0:T(4,128)S(1)}, s32[4,32]{1,0:T(4,128)}, u32[]{:S(2)}) copy-start(s32[4,32]{1,0:T(4,128)} %param.15) | copy-start | bytes 1540
  20.8 4.2 %copy-start.1 = (bf16[32,8,32]{0,2,1:T(8,128)(2,1)}, bf16[32,8,32]{0,2,1:T(8,128)(2,1)S(1)}, u32[]{:S(2)}) copy-start(bf16[32,8,32]{0,2,1:T(8,128)(2,1)S(1)} %get-tuple-element.194) | copy-start | bytes 49156 | tf_op jit(solution)/shard_map/while
  28.8 2.2 %copy-start.2 = (bf16[32,8,32]{0,2,1:T(8,128)(2,1)S(1)}, bf16[32,8,32]{0,2,1:T(8,128)(2,1)}, u32[]{:S(2)}) copy-start(bf16[32,8,32]{0,2,1:T(8,128)(2,1)} %copy-done.1) | copy-start | bytes 49156 | tf_op jit(solution)/shard_map/while
  31.0 4.2 %copy-start.1 = (bf16[32,8,32]{0,2,1:T(8,128)(2,1)}, bf16[32,8,32]{0,2,1:T(8,128)(2,1)S(1)}, u32[]{:S(2)}) copy-start(bf16[32,8,32]{0,2,1:T(8,128)(2,1)S(1)} %get-tuple-element.194) | copy-start | bytes 49156 | tf_op jit(solution)/shard_map/while
  39.0 2.2 %copy-start.2 = (bf16[32,8,32]{0,2,1:T(8,128)(2,1)S(1)}, bf16[32,8,32]{0,2,1:T(8,128)(2,1)}, u32[]{:S(2)}) copy-start(bf16[32,8,32]{0,2,1:T(8,128)(2,1)} %copy-done.1) | copy-start | bytes 49156 | tf_op jit(solution)/shard_map/while
  41.1 13.0 %copy-start.5 = (bf16[256,64]{0,1:T(8,128)(2,1)S(1)}, bf16[256,64]{0,1:T(8,128)(2,1)}, u32[]{:S(2)}) copy-start(bf16[256,64]{0,1:T(8,128)(2,1)} %param.19) | copy-start | bytes 98308
  42.9 10.3 %all-to-all-start = ((bf16[16,32,256]{2,0,1:T(8,128)(2,1)}), bf16[16,32,256]{2,0,1:T(8,128)(2,1)S(1)}, u32[]{:S(2)}, u32[]{:S(2)}) async-start(bf16[16,32,256]{2,0,1:T(8,128)(2,1)} %bitcast.140), calls=%async_computation | async-start | bytes 524288 | tf_op jit(solution)/shard_map/all_to_all | solution.py:140
  46.3 90.3 %reduce-scatter.2.cloned.1.call-start = ((), (), s32[]{:S(2)}) async-start(), calls=%async_computation.2 | async-start | bytes 294912 | tf_op jit(solution)/shard_map/reduce_scatter | solution.py:192
  66.5 1.0 copy-start.3
  66.5 1.7 %copy-start.4 = (bf16[128,384]{1,0:T(8,128)(2,1)S(1)}, bf16[128,384]{1,0:T(8,128)(2,1)}, u32[]{:S(2)}) copy-start(bf16[128,384]{1,0:T(8,128)(2,1)} %param.21) | copy-start | bytes 294916
  66.5 10.8 %copy-start.6 = (bf16[4,32,128]{2,1,0:T(8,128)(2,1)S(1)}, bf16[4,32,128]{2,1,0:T(8,128)(2,1)}, u32[]{:S(2)}) copy-start(bf16[4,32,128]{2,1,0:T(8,128)(2,1)} %param.23) | copy-start | bytes 98308
  66.5 10.8 %copy-start.8 = (bf16[128,128]{1,0:T(8,128)(2,1)S(1)}, bf16[128,128]{1,0:T(8,128)(2,1)}, u32[]{:S(2)}) copy-start(bf16[128,128]{1,0:T(8,128)(2,1)} %param.22) | copy-start | bytes 98308
  68.5 4.3 %collective-permute-start = (bf16[4,32,128]{2,1,0:T(8,128)(2,1)S(1)}, bf16[4,32,128]{2,1,0:T(8,128)(2,1)S(1)}, u32[]{:S(2)}, u32[]{:S(2)}) collective-permute-start(bf16[4,32,128]{2,1,0:T(8,128)(2,1)S(1)} %get-tuple-element.117), channel_id=1, source_target_pairs={{0,4},{4,8},{8,12},{12,16},{16,20},{20,24},{24,28},{28,0},{1,5},{5... | collective-permute-start | bytes 98312 | tf_op jit(solution)/shard_map/ppermute | solution.py:23
  72.8 4.6 %collective-permute-start.1 = (bf16[4,32,128]{2,1,0:T(8,128)(2,1)S(1)}, bf16[4,32,128]{2,1,0:T(8,128)(2,1)S(1)}, u32[]{:S(2)}, u32[]{:S(2)}) collective-permute-start(bf16[4,32,128]{2,1,0:T(8,128)(2,1)S(1)} %collective-permute-done), channel_id=1, source_target_pairs={{0,4},{4,8},{8,12},{12,16},{16,20},{20,24},{24,28},{28,0},{1,5},{5... | collective-permute-start | bytes 98312 | tf_op jit(solution)/shard_map/ppermute | solution.py:23
  72.8 5.1 %collective-permute-start.4 = (bf16[4,32,128]{2,1,0:T(8,128)(2,1)S(1)}, bf16[4,32,128]{2,1,0:T(8,128)(2,1)S(1)}, u32[]{:S(2)}, u32[]{:S(2)}) collective-permute-start(bf16[4,32,128]{2,1,0:T(8,128)(2,1)S(1)} %get-tuple-element.117), channel_id=1, source_target_pairs={{4,0},{8,4},{12,8},{16,12},{20,16},{24,20},{28,24},{0,28},{5,1},{9... | collective-permute-start | bytes 98312 | tf_op jit(solution)/shard_map/ppermute | solution.py:25
  77.3 4.2 %collective-permute-start.2 = (bf16[4,32,128]{2,1,0:T(8,128)(2,1)S(1)}, bf16[4,32,128]{2,1,0:T(8,128)(2,1)S(1)}, u32[]{:S(2)}, u32[]{:S(2)}) collective-permute-start(bf16[4,32,128]{2,1,0:T(8,128)(2,1)S(1)} %collective-permute-done.1), channel_id=1, source_target_pairs={{0,4},{4,8},{8,12},{12,16},{16,20},{20,24},{24,28},{28,0},{1,5},{5... | collective-permute-start | bytes 98312 | tf_op jit(solution)/shard_map/ppermute | solution.py:23
  77.9 14.5 %collective-permute-start.5 = (bf16[4,32,128]{2,1,0:T(8,128)(2,1)S(1)}, bf16[4,32,128]{2,1,0:T(8,128)(2,1)S(1)}, u32[]{:S(2)}, u32[]{:S(2)}) collective-permute-start(bf16[4,32,128]{2,1,0:T(8,128)(2,1)S(1)} %collective-permute-done.4), channel_id=1, source_target_pairs={{4,0},{8,4},{12,8},{16,12},{20,16},{24,20},{28,24},{0,28},{5,1},{9... | collective-permute-start | bytes 98312 | tf_op jit(solution)/shard_map/ppermute | solution.py:25
  81.6 12.5 %collective-permute-start.3 = (bf16[4,32,128]{2,1,0:T(8,128)(2,1)S(1)}, bf16[4,32,128]{2,1,0:T(8,128)(2,1)S(1)}, u32[]{:S(2)}, u32[]{:S(2)}) collective-permute-start(bf16[4,32,128]{2,1,0:T(8,128)(2,1)S(1)} %collective-permute-done.2), channel_id=1, source_target_pairs={{0,4},{4,8},{8,12},{12,16},{16,20},{20,24},{24,28},{28,0},{1,5},{5... | collective-permute-start | bytes 98312 | tf_op jit(solution)/shard_map/ppermute | solution.py:23
  92.4 3.2 %collective-permute-start.6 = (bf16[4,32,128]{2,1,0:T(8,128)(2,1)S(1)}, bf16[4,32,128]{2,1,0:T(8,128)(2,1)S(1)}, u32[]{:S(2)}, u32[]{:S(2)}) collective-permute-start(bf16[4,32,128]{2,1,0:T(8,128)(2,1)S(1)} %collective-permute-done.5), channel_id=1, source_target_pairs={{4,0},{8,4},{12,8},{16,12},{20,16},{24,20},{28,24},{0,28},{5,1},{9... | collective-permute-start | bytes 98312 | tf_op jit(solution)/shard_map/ppermute | solution.py:25
Sparse Core Ops, SparseCore 0:
  101.5 35.0 reduce-scatter.1
